TPU v7x, 32 devices: a whole 2x2x4 slice. The times are simulated.
32 devices in a mesh: wide: 8 (over z, y), narrow: 4 (over x, core).
Axes of the slice: x: 2, y: 2, z: 4, core: 2. Of those that a mesh axis runs over, the one named last changes fastest.
Arguments:
- stem: float32 [2, 8, 4, 512, 128], P(None, 'wide', 'narrow'), may hold values from -6 to 6
- branches: float32 [3, 2, 512, 512], replicated, may hold values from -0.1875 to 0.1875
- mode_order: int32 [3, 9], replicated, may hold values from 0 to 8, each once within a row
Outputs:
- final_stem: float32 [2, 8, 4, 512, 128], P(None, 'wide', 'narrow')
Inputs may be any that keep to these rules, and one draw needn't show every extreme that they name: Each row of mode_order names every mode of 0 to 8 once.
All inputs are finite; a program needn't handle non-finite values.
Results may differ from a plain program's by a relative error of at most 0.0003.
Values may be sent and summed in bfloat16 or wider, within the bound.
No kernel may reach another device: no remote copies, remote signals or barrier semaphores. Data moves between devices by JAX's collectives and lax.ppermute only.
A program may use at most 64 MiB of HBM per device.

v0:
```python
import jax
import jax.numpy as jnp
from jax import lax
from jax.sharding import PartitionSpec as P


def split_pair(values):
    high = values.astype(jnp.bfloat16)
    held = lax.optimization_barrier(high)
    low = (values - held.astype(jnp.float32)).astype(jnp.bfloat16)
    return (high, low)


def expand_order(order, columns):
    column = jnp.arange(columns, dtype=jnp.int32)
    places = jnp.arange(order.shape[0], dtype=jnp.int32)
    bits = jnp.bitwise_and(jnp.right_shift(column[:, None], places[None, :]), 1)
    return jnp.sum(jnp.left_shift(bits, order[None, :]), axis=1)


def prepare(branch_step, order):
    columns = branch_step.shape[1]
    bhigh, blow = split_pair(branch_step)
    inverse_order = jnp.argsort(order)
    inverse = expand_order(inverse_order, columns)
    return (bhigh.reshape(2 * columns, columns), blow.reshape(2 * columns, columns), inverse)


def mult(left, right):
    return lax.dot_general(
        left, right, (((0,), (0,)), ((), ())), preferred_element_type=jnp.float32
    )


def contract(stem_pieces, branch_pieces):
    shigh, slow = stem_pieces
    flat_high, flat_low, inverse = branch_pieces
    shigh = jnp.take(shigh, inverse, axis=1)
    slow = jnp.take(slow, inverse, axis=1)
    rows_count = shigh.shape[2]
    real_high = jnp.concatenate([shigh[0], -shigh[1]], axis=0)
    real_low = jnp.concatenate([slow[0], -slow[1]], axis=0)
    imag_high = jnp.concatenate([shigh[1], shigh[0]], axis=0)
    imag_low = jnp.concatenate([slow[1], slow[0]], axis=0)
    upper = mult(flat_high, jnp.concatenate([real_high, real_low, imag_high, imag_low], axis=1))
    lower = mult(flat_low, jnp.concatenate([real_high, imag_high], axis=1))
    real = upper[:, :rows_count] + upper[:, rows_count : 2 * rows_count] + lower[:, :rows_count]
    imag = (
        upper[:, 2 * rows_count : 3 * rows_count]
        + upper[:, 3 * rows_count :]
        + lower[:, rows_count:]
    )
    return jnp.stack([real, imag])


def body(stem, branches, mode_order):
    columns = stem.shape[3]
    rows_here = stem.shape[4]
    narrow_n = lax.axis_size("narrow")
    wide_n = lax.axis_size("wide")
    local = stem.reshape(2, columns, rows_here)
    first_branch = prepare(branches[0], mode_order[0])
    second_branch = prepare(branches[1], mode_order[1])
    third_branch = prepare(branches[2], mode_order[2])
    first = contract(split_pair(local), first_branch)
    outgoing = first.reshape(2, narrow_n, columns // narrow_n, rows_here)
    received = lax.all_to_all(outgoing, "narrow", split_axis=1, concat_axis=1, tiled=True)
    merged = received.reshape(2, columns, received.shape[3])
    second = contract(split_pair(merged), second_branch)
    outgoing = second.reshape(2, wide_n, columns // wide_n, rows_here)
    received = lax.all_to_all(outgoing, "wide", split_axis=1, concat_axis=1, tiled=True)
    merged = received.reshape(2, columns, received.shape[3])
    final = contract(split_pair(merged), third_branch)
    return final.reshape(2, 1, 1, columns, rows_here)


def solution(mesh):
    return jax.shard_map(
        body,
        mesh=mesh,
        in_specs=(P(None, "wide", "narrow", None, None), P(), P()),
        out_specs=P(None, "wide", "narrow", None, None),
        check_vma=False,
    )
```

profile of v0, /device:TPU:0, one launch (start us, length us, event | category | flops | bytes accessed | tf_op | source)
XLA Modules:
  0.0 81.4 jit_solution(7135167233199474065)
XLA Ops:
  0.0 0.8 slice_bitcast_fusion
  0.8 1.3 %sort.45 = (s32[9]{0:T(128)}, s32[9]{0:T(128)S(1)}) sort(s32[9]{0:T(128)S(1)} %get-tuple-element.52, s32[9]{0:T(128)S(1)} %iota.22), dimensions={0}, to_apply=%region_0.0 | sort | flops 36 | bytes 144 | tf_op jit(solution)/shard_map/jit(argsort)/sort | solution.py:24
  2.1 0.1 shift-left_reduce_fusion.2
  2.2 0.0 copy-start
  2.2 4.9 %fusion.95 = (bf16[1,2,512,512]{3,2,1,0:T(8,128)(2,1)}, bf16[2,512,512]{2,1,0:T(8,128)(2,1)S(1)}, bf16[2,512,512]{2,1,0:T(8,128)(2,1)S(1)}, bf16[2,512,512]{2,1,...) fusion(f32[3,2,512,512]{3,2,1,0:T(8,128)} %param.6), kind=kLoop, calls=%fused_computation.168 | loop fusion | bytes 9437184 | tf_op jit(solution)/shard_map/slice | solution.py:64
  7.0 0.0 copy-done
  7.0 0.4 copy.102
  7.4 1.2 %fusion.74 = bf16[2,512,128]{2,0,1:T(2,128)(2,1)} fusion(bf16[2,512,128]{2,0,1:T(2,128)(2,1)S(1)} %bitcast.121, f32[2,1,1,512,128]{4,3,2,1,0:T(8,128)S(1)} %copy-done), kind=kLoop, calls=%fused_computation.101 | loop fusion | flops 393216 | bytes 1048576 | tf_op jit(solution)/shard_map/convert_element_type | solution.py:10
  8.6 2.4 %gather_fusion = bf16[512,2,128]{2,1,0:T(2,128)(2,1)} fusion(bf16[2,512,128]{2,0,1:T(2,128)(2,1)S(1)} %bitcast.122, s32[1024]{0:T(1024)S(1)} %pad_clamp_fusion.2), kind=kCustom, calls=%fused_computation.clone | custom fusion | bytes 526336 | tf_op jit(solution)/shard_map/jit(_take)/gather | solution.py:38
  11.0 2.3 %gather_fusion.1 = bf16[512,2,128]{2,1,0:T(2,128)(2,1)S(1)} fusion(bf16[2,512,128]{2,0,1:T(2,128)(2,1)} %fusion.74, s32[1024]{0:T(1024)S(1)} %pad_clamp_fusion.2), kind=kCustom, calls=%fused_computation.1.clone | custom fusion | bytes 526336 | tf_op jit(solution)/shard_map/jit(_take)/gather | solution.py:39
  13.3 3.0 %fusion.78 = (bf16[2,512,128]{2,0,1:T(2,128)(2,1)S(1)}, bf16[2,512,128]{2,0,1:T(2,128)(2,1)S(1)}) fusion(bf16[512,2,128]{2,1,0:T(2,128)(2,1)S(1)} %gather_fusion.1, pred[512]{0:T(512)(128)(4,1)S(1)} %compare_and_fusion.2, bf16[512,2,128]{2,1,0:T(2,128)(2,1)} %gather_fusion), kind=kLoop, calls=%fused_computation.123 | loop fusion | flops 262144 | bytes 1049088 | tf_op jit(solution)/shard_map/jit(_take)/select_n | solution.py:39
  16.3 0.7 fusion.100
  17.2 5.3 %fusion.2 = (bf16[2,512,512]{2,1,0:T(8,128)(2,1)S(1)}, bf16[2,512,512]{2,1,0:T(8,128)(2,1)}, bf16[2,512,512]{2,1,0:T(8,128)(2,1)}) fusion(bf16[2,512,512]{2,1,0:T(8,128)(2,1)S(1)} %get-tuple-element.25, f32[3,2,512,512]{3,2,1,0:T(8,128)} %param.6, bf16[2,512,512]{2,1,0:T(8,128)(2,1)S(1)} %get-tuple-element.26, bf16[2,512,512]{2,1,0:T(8,128)(2,1)S(1)} %get-tuple-element.27), kind=kLoop, calls=%fused_computation.14 | loop fusion | flops 4718592 | bytes 12582912 | tf_op jit(solution)/shard_map/convert_element_type | solution.py:10
  22.5 0.0 copy-start.5
  22.5 0.5 fusion.48
  23.0 0.7 copy-done.5
  23.7 0.8 convolution_bitcast_fusion.2
  24.5 0.1 slice_add_fusion.10
  24.6 0.8 %pad_maximum_fusion = f32[2,4,128,128]{3,2,0,1:T(8,128)} fusion(f32[1,4,128,128]{3,2,0,1:T(8,128)S(1)} %bitcast.130, f32[1,4,128,128]{3,2,0,1:T(8,128)S(1)} %bitcast.129), kind=kLoop, calls=%fused_computation.74 | loop fusion | flops 131072 | bytes 1048576 | tf_op jit(solution)/shard_map/stack | solution.py:53
  25.4 4.2 %all-to-all-start = ((f32[2,4,128,128]{3,2,0,1:T(8,128)}), f32[2,4,128,128]{3,2,0,1:T(8,128)S(1)}, u32[]{:S(2)}, u32[]{:S(2)}) async-start(f32[2,4,128,128]{3,2,0,1:T(8,128)} %pad_maximum_fusion), calls=%async_computation | async-start | bytes 1048576 | tf_op jit(solution)/shard_map/all_to_all | solution.py:67
  29.6 1.2 %sort.46 = (s32[9]{0:T(128)}, s32[9]{0:T(128)S(1)}) sort(s32[9]{0:T(128)S(1)} %get-tuple-element.53, s32[9]{0:T(128)S(1)} %iota.23), dimensions={0}, to_apply=%region_2.0 | sort | flops 36 | bytes 144 | tf_op jit(solution)/shard_map/jit(argsort)/sort | solution.py:24
  30.8 0.1 shift-left_reduce_fusion.1
  31.0 7.5 %all-to-all-done = f32[2,4,128,128]{3,2,0,1:T(8,128)S(1)} async-done(((f32[2,4,128,128]{3,2,0,1:T(8,128)}), f32[2,4,128,128]{3,2,0,1:T(8,128)S(1)}, u32[]{:S(2)}, u32[]{:S(2)}) %all-to-all-start) | async-done | bytes 524320 | tf_op jit(solution)/shard_map/all_to_all | solution.py:67
  38.5 0.4 copy.62
  38.9 0.2 bitcast_convert_fusion.4
  39.1 0.3 fusion.73
  39.4 2.1 %gather_fusion.2 = bf16[512,2,128]{2,1,0:T(2,128)(2,1)S(1)} fusion(bf16[2,512,128]{2,0,1:T(2,128)(2,1)S(1)} %bitcast_convert_fusion.4, s32[1024]{0:T(1024)S(1)} %pad_clamp_fusion.1), kind=kCustom, calls=%fused_computation.2.clone | custom fusion | bytes 526336 | tf_op jit(solution)/shard_map/jit(_take)/gather | solution.py:38
  41.6 2.1 %gather_fusion.3 = bf16[512,2,128]{2,1,0:T(2,128)(2,1)S(1)} fusion(bf16[2,512,128]{2,0,1:T(2,128)(2,1)S(1)} %fusion.73, s32[1024]{0:T(1024)S(1)} %pad_clamp_fusion.1), kind=kCustom, calls=%fused_computation.3.clone | custom fusion | bytes 526336 | tf_op jit(solution)/shard_map/jit(_take)/gather | solution.py:39
  43.7 1.8 %fusion.80 = (bf16[2,512,128]{2,0,1:T(2,128)(2,1)S(1)}, bf16[2,512,128]{2,0,1:T(2,128)(2,1)S(1)}) fusion(bf16[512,2,128]{2,1,0:T(2,128)(2,1)S(1)} %gather_fusion.3, pred[512]{0:T(512)(128)(4,1)S(1)} %compare_and_fusion.1, bf16[512,2,128]{2,1,0:T(2,128)(2,1)S(1)} %gather_fusion.2), kind=kLoop, calls=%fused_computation.125 | loop fusion | flops 262144 | bytes 1049088 | tf_op jit(solution)/shard_map/jit(_take)/select_n | solution.py:39
  45.5 0.0 copy-start.4
  45.5 0.4 fusion.99
  45.9 0.4 fusion.98
  46.3 0.0 copy-start.3
  46.4 0.3 copy-done.4
  46.7 0.5 fusion.56
  47.2 0.4 copy-done.3
  47.6 0.7 convolution_bitcast_fusion.1
  48.4 0.1 slice_add_fusion.6
  48.5 0.8 %pad_maximum_fusion.1 = f32[2,8,64,128]{3,2,0,1:T(8,128)} fusion(f32[1,8,64,128]{3,2,0,1:T(8,128)S(1)} %bitcast.132, f32[1,8,64,128]{3,2,0,1:T(8,128)S(1)} %bitcast.131), kind=kLoop, calls=%fused_computation.83 | loop fusion | flops 131072 | bytes 1048576 | tf_op jit(solution)/shard_map/stack | solution.py:53
  49.3 6.5 %all-to-all-start.1 = ((f32[2,8,64,128]{3,2,0,1:T(8,128)}), f32[2,8,64,128]{3,2,0,1:T(8,128)S(1)}, u32[]{:S(2)}, u32[]{:S(2)}) async-start(f32[2,8,64,128]{3,2,0,1:T(8,128)} %pad_maximum_fusion.1), calls=%async_computation.1 | async-start | bytes 1048576 | tf_op jit(solution)/shard_map/all_to_all | solution.py:71
  55.8 1.3 %sort.47 = (s32[9]{0:T(128)}, s32[9]{0:T(128)S(1)}) sort(s32[9]{0:T(128)S(1)} %get-tuple-element.51, s32[9]{0:T(128)S(1)} %iota.24), dimensions={0}, to_apply=%region_4.6 | sort | flops 36 | bytes 144 | tf_op jit(solution)/shard_map/jit(argsort)/sort | solution.py:24
  57.1 0.1 shift-left_reduce_fusion
  57.2 12.8 %all-to-all-done.1 = f32[2,8,64,128]{3,2,0,1:T(8,128)S(1)} async-done(((f32[2,8,64,128]{3,2,0,1:T(8,128)}), f32[2,8,64,128]{3,2,0,1:T(8,128)S(1)}, u32[]{:S(2)}, u32[]{:S(2)}) %all-to-all-start.1) | async-done | bytes 524320 | tf_op jit(solution)/shard_map/all_to_all | solution.py:71
  70.0 0.4 copy.65
  70.4 0.2 bitcast_convert_fusion.3
  70.7 0.3 fusion.72
  71.0 2.1 %gather_fusion.4 = bf16[512,2,128]{2,1,0:T(2,128)(2,1)S(1)} fusion(bf16[2,512,128]{2,0,1:T(2,128)(2,1)S(1)} %bitcast_convert_fusion.3, s32[1024]{0:T(1024)S(1)} %pad_clamp_fusion), kind=kCustom, calls=%fused_computation.4.clone | custom fusion | bytes 526336 | tf_op jit(solution)/shard_map/jit(_take)/gather | solution.py:38
  73.1 2.1 %gather_fusion.5 = bf16[512,2,128]{2,1,0:T(2,128)(2,1)S(1)} fusion(bf16[2,512,128]{2,0,1:T(2,128)(2,1)S(1)} %fusion.72, s32[1024]{0:T(1024)S(1)} %pad_clamp_fusion), kind=kCustom, calls=%fused_computation.5.clone | custom fusion | bytes 526336 | tf_op jit(solution)/shard_map/jit(_take)/gather | solution.py:39
  75.2 1.8 %fusion.82 = (bf16[2,512,128]{2,0,1:T(2,128)(2,1)S(1)}, bf16[2,512,128]{2,0,1:T(2,128)(2,1)S(1)}) fusion(bf16[512,2,128]{2,1,0:T(2,128)(2,1)S(1)} %gather_fusion.5, pred[512]{0:T(512)(128)(4,1)S(1)} %compare_and_fusion, bf16[512,2,128]{2,1,0:T(2,128)(2,1)S(1)} %gather_fusion.4), kind=kLoop, calls=%fused_computation.127 | loop fusion | flops 262144 | bytes 1049088 | tf_op jit(solution)/shard_map/jit(_take)/select_n | solution.py:39
  77.0 0.0 copy-start.2
  77.0 0.4 fusion.97
  77.5 0.4 fusion.96
  77.9 0.3 copy-done.2
  78.2 0.0 copy-start.1
  78.2 0.5 fusion.64
  78.7 0.7 copy-done.1
  79.5 0.7 convolution_bitcast_fusion
  80.2 0.1 fusion.76
  80.4 1.0 %copy.68 = f32[2,1,1,512,128]{4,3,2,1,0:T(8,128)} copy(f32[2,1,1,512,128]{3,4,0,2,1:T(8,128)S(1)} %maximum_bitcast_fusion) | data formatting | bytes 1048576 | tf_op jit(solution)/shard_map/reshape | solution.py:74
  (25 shorter events, 0.5 us)
Async XLA Ops:
  2.2 4.9 %copy-start = (f32[2,1,1,512,128]{4,3,2,1,0:T(8,128)S(1)}, f32[2,1,1,512,128]{4,3,2,1,0:T(8,128)}, u32[]{:S(2)}) copy-start(f32[2,1,1,512,128]{4,3,2,1,0:T(8,128)} %param.5) | copy-start | bytes 1572868
  22.5 1.2 %copy-start.5 = (bf16[1,2,512,512]{3,2,1,0:T(8,128)(2,1)S(1)}, bf16[1,2,512,512]{3,2,1,0:T(8,128)(2,1)}, u32[]{:S(2)}) copy-start(bf16[1,2,512,512]{3,2,1,0:T(8,128)(2,1)} %get-tuple-element.28) | copy-start | bytes 3145732
  25.4 13.1 %all-to-all-start = ((f32[2,4,128,128]{3,2,0,1:T(8,128)}), f32[2,4,128,128]{3,2,0,1:T(8,128)S(1)}, u32[]{:S(2)}, u32[]{:S(2)}) async-start(f32[2,4,128,128]{3,2,0,1:T(8,128)} %pad_maximum_fusion), calls=%async_computation | async-start | bytes 1048576 | tf_op jit(solution)/shard_map/all_to_all | solution.py:67
  45.5 1.2 %copy-start.4 = (bf16[2,512,512]{2,1,0:T(8,128)(2,1)S(1)}, bf16[2,512,512]{2,1,0:T(8,128)(2,1)}, u32[]{:S(2)}) copy-start(bf16[2,512,512]{2,1,0:T(8,128)(2,1)} %get-tuple-element.31) | copy-start | bytes 3145732
  46.3 1.3 %copy-start.3 = (bf16[1,2,512,512]{3,2,1,0:T(8,128)(2,1)S(1)}, bf16[1,2,512,512]{3,2,1,0:T(8,128)(2,1)}, u32[]{:S(2)}) copy-start(bf16[1,2,512,512]{3,2,1,0:T(8,128)(2,1)} %get-tuple-element.29) | copy-start | bytes 3145732
  49.3 20.7 %all-to-all-start.1 = ((f32[2,8,64,128]{3,2,0,1:T(8,128)}), f32[2,8,64,128]{3,2,0,1:T(8,128)S(1)}, u32[]{:S(2)}, u32[]{:S(2)}) async-start(f32[2,8,64,128]{3,2,0,1:T(8,128)} %pad_maximum_fusion.1), calls=%async_computation.1 | async-start | bytes 1048576 | tf_op jit(solution)/shard_map/all_to_all | solution.py:71
  77.0 1.2 %copy-start.2 = (bf16[2,512,512]{2,1,0:T(8,128)(2,1)S(1)}, bf16[2,512,512]{2,1,0:T(8,128)(2,1)}, u32[]{:S(2)}) copy-start(bf16[2,512,512]{2,1,0:T(8,128)(2,1)} %get-tuple-element.32) | copy-start | bytes 3145732
  78.2 1.2 %copy-start.1 = (bf16[1,2,512,512]{3,2,1,0:T(8,128)(2,1)S(1)}, bf16[1,2,512,512]{3,2,1,0:T(8,128)(2,1)}, u32[]{:S(2)}) copy-start(bf16[1,2,512,512]{3,2,1,0:T(8,128)(2,1)} %get-tuple-element.24) | copy-start | bytes 3145732
where the time goes:
time: 81.9 us; the launch traced here: 81.4 us
  local copies, waits for them, and re-layouts  25.9 us (32%)
  other arithmetic  20.5 us (25%)
  waiting for transfers between devices  20.3 us (25%)
  starting transfers between devices  10.7 us (13%)
  matrix products  3.67 us (4%)
    all_to_all x1, waiting for transfers between devices, body(): lax.all_to_all(outgoing, 'wide', split_axis=1, concat_axis=1, tiled=True)  12.8 us
    all_to_all x1, waiting for transfers between devices, body(): lax.all_to_all(outgoing, 'narrow', split_axis=1, concat_axis=1, tiled=True)  7.53 us
    convert_element_type x4, other arithmetic, split_pair(): low = (values - held.astype(jnp.float32)).astype(jnp.bfloat16)  7.11 us
    gather x3, local copies, waits for them, and re-layouts, contract(): shigh = jnp.take(shigh, inverse, axis=1)  6.6 us
    select_n x3, other arithmetic, contract(): slow = jnp.take(slow, inverse, axis=1)  6.55 us
    gather x3, local copies, waits for them, and re-layouts, contract(): slow = jnp.take(slow, inverse, axis=1)  6.53 us
    all_to_all x1, starting transfers between devices, body(): lax.all_to_all(outgoing, 'wide', split_axis=1, concat_axis=1, tiled=True)  6.47 us
    slice x1, local copies, waits for them, and re-layouts, body(): third_branch = prepare(branches[2], mode_order[2])  4.86 us
  transfers between devices with their start and end apart: 2, of which 2 were waited for; matrix products, arithmetic and copies ran while one was open for 3% of the time, Pallas kernels for 0%

commit v1 on v0

v1 whole, which is shorter than its diff:
```python
import functools

import jax
import jax.numpy as jnp
from jax import lax
from jax.experimental import pallas as pl
from jax.experimental.pallas import tpu as pltpu
from jax.sharding import PartitionSpec as P

LANES = 128
SUBLANES = 8
TOP = 32767.0
FINE = 65536.0


def split_pair(values):
    high = values.astype(jnp.bfloat16)
    low = (values - high.astype(jnp.float32)).astype(jnp.bfloat16)
    return high, low


def dot(left, right):
    return lax.dot_general(left, right, (((1,), (0,)), ((), ())), preferred_element_type=jnp.float32)


def one_hot(order_ref, step, columns):
    row = lax.broadcasted_iota(jnp.int32, (SUBLANES, columns), 1)
    meets = jnp.zeros_like(row)
    for b in range(order_ref.shape[1]):
        bit = jnp.bitwise_and(jnp.right_shift(row, order_ref[step, b]), 1)
        meets = meets + jnp.left_shift(bit, b)
    column = lax.broadcasted_iota(jnp.int32, (columns, columns), 0)
    return jnp.where(column == meets[0:1, :], 1.0, 0.0).astype(jnp.bfloat16)


def fetch(step, branches_ref, held, sems):
    parts = held.shape[0]
    size = held.shape[2]
    copies = []
    for p in range(parts):
        copy = pltpu.make_async_copy(
            branches_ref.at[step, :, pl.ds(p * size, size), :], held.at[p], sems.at[p]
        )
        copy.start()
        copies.append(copy)
    return copies


def contract(order_ref, step, real, imag, held, copies):
    rows, columns = real.shape
    real_high, real_low = split_pair(real)
    imag_high, imag_low = split_pair(imag)
    pieces = jnp.concatenate([real_high, imag_high, real_low, imag_low], axis=0)
    moved = dot(pieces, one_hot(order_ref, step, columns)).astype(jnp.bfloat16)
    real_high, imag_high, real_low, imag_low = (moved[q * rows : (q + 1) * rows] for q in range(4))
    plain = jnp.concatenate([real_high, imag_high, real_low, imag_low], axis=0)
    turned = jnp.concatenate([-imag_high, real_high, -imag_low, real_low], axis=0)
    size = held.shape[2]
    wide_sum = jnp.zeros((4 * rows, columns), jnp.float32)
    high_sum = jnp.zeros((2 * rows, columns), jnp.float32)
    for p, copy in enumerate(copies):
        copy.wait()
        part = slice(p * size, (p + 1) * size)
        r_high, r_low = split_pair(held[p, 0])
        i_high, i_low = split_pair(held[p, 1])
        wide_sum = wide_sum + dot(plain[:, part], r_high) + dot(turned[:, part], i_high)
        high_sum = high_sum + dot(plain[: 2 * rows, part], r_low) + dot(turned[: 2 * rows, part], i_low)
    return wide_sum[: 2 * rows] + wide_sum[2 * rows :] + high_sum


def lane_block(shape, width):
    return lax.broadcasted_iota(jnp.int32, shape, 1) // width


def rotate(values, amount):
    amount = amount % LANES
    return pltpu.roll(values, amount, 1) if amount else values


def encode(out_ref, slot, real, imag):
    rows = real.shape[0]
    tall = jnp.maximum(jnp.abs(real), jnp.abs(imag)).reshape(rows // SUBLANES, SUBLANES, LANES)
    largest = jnp.maximum(jnp.max(tall, axis=0), 1e-30)
    level = jnp.ceil(jnp.log2(largest) * FINE)
    gain = jnp.exp2(level * (-1.0 / FINE)) * (TOP - 1.0)
    gain = jnp.broadcast_to(gain[None], tall.shape).reshape(rows, LANES)
    upper = jnp.round(real * gain).astype(jnp.int32)
    lower = jnp.round(imag * gain).astype(jnp.int32)
    out_ref[slot, 0:rows, :] = jnp.bitwise_or(jnp.left_shift(upper, 16), jnp.bitwise_and(lower, 0xFFFF))
    out_ref[slot, rows : rows + SUBLANES, :] = level.astype(jnp.int32)


def decode(in_ref, slot):
    rows = in_ref.shape[1] - SUBLANES
    codes = in_ref[slot, 0:rows, :]
    level = in_ref[slot, rows : rows + SUBLANES, :].astype(jnp.float32)
    step = jnp.exp2(level * (1.0 / FINE)) * (1.0 / (TOP - 1.0))
    step = jnp.broadcast_to(step[None], (rows // SUBLANES, SUBLANES, LANES)).reshape(rows, LANES)
    real = jnp.right_shift(codes, 16).astype(jnp.float32) * step
    imag = jnp.right_shift(jnp.left_shift(codes, 16), 16).astype(jnp.float32) * step
    return real, imag


def pack(out_ref, sums):
    blocks = out_ref.shape[0]
    rows = sums.shape[0] // 2
    width = sums.shape[1] // blocks
    share = LANES // width
    height = rows // share
    for tile in range(sums.shape[1] // LANES):
        lanes = slice(tile * LANES, (tile + 1) * LANES)
        both = (sums[:rows, lanes], sums[rows:, lanes])
        for p in range(share):
            made = []
            for values in both:
                piece = rotate(values[0:height], -p * width)
                for q in range(1, share):
                    other = rotate(values[q * height : (q + 1) * height], (q - p) * width)
                    piece = jnp.where(lane_block(other.shape, width) == q, other, piece)
                made.append(piece)
            encode(out_ref, tile * share + p, *made)


def unpack(in_ref, rows, columns):
    blocks = in_ref.shape[0]
    width = columns // blocks
    share = LANES // width
    tiles = []
    for tile in range(columns // LANES):
        got = [decode(in_ref, tile * share + p) for p in range(share)]
        both = []
        for c in range(2):
            groups = []
            for q in range(share):
                piece = rotate(got[0][c], -q * width)
                for p in range(1, share):
                    other = rotate(got[p][c], (p - q) * width)
                    piece = jnp.where(lane_block(other.shape, width) == p, other, piece)
                groups.append(piece)
            both.append(jnp.concatenate(groups, axis=0) if share > 1 else groups[0])
        tiles.append(both)
    return tuple(jnp.concatenate([t[c] for t in tiles], axis=1) for c in range(2))


def first_kernel(order_ref, stem_ref, branches_ref, out_ref, held, sems):
    copies = fetch(0, branches_ref, held, sems)
    real, imag = stem_ref[0].T, stem_ref[1].T
    pack(out_ref, contract(order_ref, 0, real, imag, held, copies))


def middle_kernel(order_ref, in_ref, branches_ref, out_ref, held, sems):
    copies = fetch(1, branches_ref, held, sems)
    columns = held.shape[3]
    rows = (in_ref.shape[1] - SUBLANES) * in_ref.shape[0] * LANES // columns
    real, imag = unpack(in_ref, rows, columns)
    pack(out_ref, contract(order_ref, 1, real, imag, held, copies))


def last_kernel(order_ref, in_ref, branches_ref, out_ref, held, sems):
    copies = fetch(2, branches_ref, held, sems)
    columns = held.shape[3]
    rows = (in_ref.shape[1] - SUBLANES) * in_ref.shape[0] * LANES // columns
    real, imag = unpack(in_ref, rows, columns)
    sums = contract(order_ref, 2, real, imag, held, copies)
    out_ref[0] = sums[:rows].T
    out_ref[1] = sums[rows:].T


PARTS = 2


def call(kernel, out_shape, order, data, branches):
    columns = branches.shape[3]
    return pl.pallas_call(
        kernel,
        out_shape=out_shape,
        in_specs=[
            pl.BlockSpec(memory_space=pltpu.SMEM),
            pl.BlockSpec(memory_space=pltpu.VMEM),
            pl.BlockSpec(memory_space=pl.ANY),
        ],
        out_specs=pl.BlockSpec(memory_space=pltpu.VMEM),
        scratch_shapes=[
            pltpu.VMEM((PARTS, 2, columns // PARTS, columns), jnp.float32),
            pltpu.SemaphoreType.DMA((PARTS,)),
        ],
        compiler_params=pltpu.CompilerParams(vmem_limit_bytes=32 << 20),
    )(order, data, branches)


def body(stem, branches, mode_order):
    columns, rows = stem.shape[3:]
    local = stem.reshape(2, columns, rows)

    def coded(blocks):
        return jax.ShapeDtypeStruct((blocks, rows * columns // blocks // LANES + SUBLANES, LANES), jnp.int32)

    swap = functools.partial(lax.all_to_all, split_axis=0, concat_axis=0, tiled=True)
    first = call(first_kernel, coded(lax.axis_size("narrow")), mode_order, local, branches)
    first = swap(first, "narrow")
    second = call(middle_kernel, coded(lax.axis_size("wide")), mode_order, first, branches)
    second = swap(second, "wide")
    final = call(last_kernel, jax.ShapeDtypeStruct((2, columns, rows), jnp.float32), mode_order, second, branches)
    return final.reshape(2, 1, 1, columns, rows)


def solution(mesh):
    return jax.shard_map(
        body,
        mesh=mesh,
        in_specs=(P(None, "wide", "narrow", None, None), P(), P()),
        out_specs=P(None, "wide", "narrow", None, None),
        check_vma=False,
    )
```

time: 81.9 us -> 39.2 us (0.48)
  blocking collectives: 0 us -> 26.4 us
  local copies, waits for them, and re-layouts: 25.9 us -> 4.51 us
  other arithmetic: 20.5 us -> 0 us
  waiting for transfers between devices: 20.3 us -> 0 us
  starting transfers between devices: 10.7 us -> 0 us
  Pallas kernels: 0 us -> 7.98 us
  matrix products: 3.67 us -> 0 us
    all_to_all x0 -> x2, blocking collectives: none -> 26.4 us  [the longest x1 16.2 us: body(): second = swap(second, 'wide')]
    all_to_all x2 -> x0, waiting for transfers between devices: 20.3 us -> none  [the longest x1 12.8 us: body(): lax.all_to_all(outgoing, 'wide', split_axis=1, concat_axis=1, tiled=True)]
    gather x6 -> x0, local copies, waits for them, and re-layouts: 13.1 us -> none  [the longest x3 6.6 us: contract(): shigh = jnp.take(shigh, inverse, axis=1)]
    all_to_all x2 -> x0, starting transfers between devices: 10.7 us -> none  [the longest x1 6.47 us: body(): lax.all_to_all(outgoing, 'wide', split_axis=1, concat_axis=1, tiled=True)]
    pallas_call x0 -> x3, Pallas kernels: none -> 7.98 us  [call(): pl.pallas_call(kernel, out_shape=out_shape, in_specs=[pl.BlockSpec(memory...]
    convert_element_type x6 -> x0, other arithmetic: 7.54 us -> none  [the longest x4 7.11 us: split_pair(): low = (values - held.astype(jnp.float32)).astype(jnp.bfloat16)]
    slice x6 -> x0, local copies, waits for them, and re-layouts: 7.06 us -> none  [the longest x1 4.86 us: body(): third_branch = prepare(branches[2], mode_order[2])]
    select_n x6 -> x0, other arithmetic: 6.57 us -> none  [the longest x3 6.55 us: contract(): slow = jnp.take(slow, inverse, axis=1)]
  transfers between devices with their start and end apart: 2 -> 0, of which waited for: 2 -> 0; matrix products, arithmetic and copies ran while one was open for 3% -> 0% of each run, Pallas kernels for 0% -> 0%
where the time goes in v1:
time: 39.2 us; the launch traced here: 38.9 us
  blocking collectives  26.4 us (67%)
  Pallas kernels  7.98 us (20%)
  local copies, waits for them, and re-layouts  4.51 us (12%)
    all_to_all x1, blocking collectives, body(): second = swap(second, 'wide')  16.2 us
    all_to_all x1, blocking collectives, body(): first = swap(first, 'narrow')  10.2 us
    pallas_call x3, Pallas kernels, call(): pl.pallas_call(kernel, out_shape=out_shape, in_specs=[pl.BlockSpec(memory...  7.98 us
    unnamed x8, local copies, waits for them, and re-layouts  4.51 us

profile of v1, /device:TPU:0, one launch (start us, length us, event | category | flops | bytes accessed | tf_op | source)
XLA Modules:
  0.0 38.9 jit_solution(9647382461451818601)
XLA Ops:
  0.0 0.0 copy-start
  0.0 2.8 %copy-done = f32[3,2,512,512]{3,2,1,0:T(8,128)S(1)} copy-done((f32[3,2,512,512]{3,2,1,0:T(8,128)S(1)}, f32[3,2,512,512]{3,2,1,0:T(8,128)}, u32[]{:S(2)}) %copy-start) | copy-done | bytes 6291480
  2.8 0.0 copy-start.2
  2.8 1.0 %copy-done.2 = f32[2,1,1,512,128]{4,3,2,1,0:T(8,128)S(1)} copy-done((f32[2,1,1,512,128]{4,3,2,1,0:T(8,128)S(1)}, f32[2,1,1,512,128]{4,3,2,1,0:T(8,128)}, u32[]{:S(2)}) %copy-start.2) | copy-done | bytes 524312
  3.8 0.0 copy-start.3
  3.8 0.7 %copy-done.3 = s32[3,9]{1,0:T(4,128)S(1)} copy-done((s32[3,9]{1,0:T(4,128)S(1)}, s32[3,9]{1,0:T(4,128)}, u32[]{:S(2)}) %copy-start.3) | copy-done | bytes 132
  4.5 0.0 copy-start.1
  4.5 2.3 %shard_map.37 = s32[4,136,128]{2,1,0:T(8,128)S(1)} custom-call(s32[3,9]{1,0:T(4,128)S(1)} %copy-done.3, f32[2,512,128]{2,1,0:T(8,128)S(1)} %bitcast.4, f32[3,2,512,512]{3,2,1,0:T(8,128)S(1)} %copy-done), custom_call_target="tpu_custom_call" | custom-call | tf_op jit(solution)/shard_map/pallas_call | solution.py:174
  6.8 10.2 %all_to_all.10.in_ref = s32[4,136,128]{2,1,0:T(8,128)S(1)} all-to-all(s32[4,136,128]{2,1,0:T(8,128)S(1)} %shard_map.37), channel_id=1, replica_groups=mesh['wide'=8,'narrow'=4] {'narrow'}, dimensions={0} | all-to-all | bytes 557056 | tf_op jit(solution)/shard_map/all_to_all | solution.py:200
  17.1 0.0 copy-done.1
  17.1 2.4 %shard_map.38 = s32[8,72,128]{2,1,0:T(8,128)S(1)} custom-call(s32[3,9]{1,0:T(4,128)S(1)} %copy-done.3, s32[4,136,128]{2,1,0:T(8,128)S(1)} %all_to_all.10.in_ref, f32[3,2,512,512]{3,2,1,0:T(8,128)S(1)} %copy-done.1), custom_call_target="tpu_custom_call" | custom-call | tf_op jit(solution)/shard_map/pallas_call | solution.py:174
  19.5 16.2 %all_to_all.11.in_ref = s32[8,72,128]{2,1,0:T(8,128)S(1)} all-to-all(s32[8,72,128]{2,1,0:T(8,128)S(1)} %shard_map.38), channel_id=1, replica_groups=mesh['wide'=8,'narrow'=4] {'wide'}, dimensions={0} | all-to-all | bytes 589824 | tf_op jit(solution)/shard_map/all_to_all | solution.py:202
  35.7 3.2 %shard_map.39 = f32[2,512,128]{2,1,0:T(8,128)} custom-call(s32[3,9]{1,0:T(4,128)S(1)} %copy-done.3, s32[8,72,128]{2,1,0:T(8,128)S(1)} %all_to_all.11.in_ref, f32[3,2,512,512]{3,2,1,0:T(8,128)S(1)} %copy-done.1), custom_call_target="tpu_custom_call" | custom-call | tf_op jit(solution)/shard_map/pallas_call | solution.py:174
Async XLA Ops:
  0.0 2.8 %copy-start = (f32[3,2,512,512]{3,2,1,0:T(8,128)S(1)}, f32[3,2,512,512]{3,2,1,0:T(8,128)}, u32[]{:S(2)}) copy-start(f32[3,2,512,512]{3,2,1,0:T(8,128)} %branches_ref.5) | copy-start | bytes 18874372
  2.8 1.0 %copy-start.2 = (f32[2,1,1,512,128]{4,3,2,1,0:T(8,128)S(1)}, f32[2,1,1,512,128]{4,3,2,1,0:T(8,128)}, u32[]{:S(2)}) copy-start(f32[2,1,1,512,128]{4,3,2,1,0:T(8,128)} %param.3) | copy-start | bytes 1572868
  3.8 0.7 %copy-start.3 = (s32[3,9]{1,0:T(4,128)S(1)}, s32[3,9]{1,0:T(4,128)}, u32[]{:S(2)}) copy-start(s32[3,9]{1,0:T(4,128)} %order_ref.5) | copy-start | bytes 328
  4.5 12.6 %copy-start.1 = (f32[3,2,512,512]{3,2,1,0:T(8,128)S(1)}, f32[3,2,512,512]{3,2,1,0:T(8,128)}, u32[]{:S(2)}) copy-start(f32[3,2,512,512]{3,2,1,0:T(8,128)} %branches_ref.5) | copy-start | bytes 18874372
